TPU v7x, 128 devices: a whole 4x4x4 slice. The times are simulated.
128 devices in a mesh: row: 8 (over x, z_hi), col: 16 (over y, z_lo, core).
Axes of the slice: x: 4, y: 4, z: 4 (z_hi: 2, z_lo: 2; z = z_hi * 2 + z_lo), core: 2. Of those that a mesh axis runs over, the one named last changes fastest.
Arguments:
- grad_out: bfloat16 [16, 256, 8192], P('col', 'row'), may hold values from -0.25 to 0.25
- pre_act: bfloat16 [4096, 14336], P('col', 'row'), may hold values from -6 to 6
- down_weight: bfloat16 [8192, 14336], P('col', 'row'), may hold values from -3 to 3
Outputs:
- grad_pre: bfloat16 [4096, 14336], P('col', 'row')
- grad_weight: bfloat16 [8192, 14336], P('col', 'row')
All inputs are finite; a program needn't handle non-finite values.
Results may differ from a plain program's by a relative error of at most 0.0048.
Values may be sent and summed in bfloat16 or wider, within the bound.
No kernel may reach another device: no remote copies, remote signals or barrier semaphores. Data moves between devices by JAX's collectives and lax.ppermute only.
A program may use at most 128 MiB of HBM per device.

v0:
```python
import math
import jax
import jax.numpy as jnp
from jax import lax
from jax.sharding import PartitionSpec as P


def gelu_parts(pre_float):
    cumulative = 0.5 * (1.0 + jax.scipy.special.erf(pre_float / math.sqrt(2.0)))
    density = jnp.exp(-0.5 * pre_float * pre_float) / math.sqrt(2.0 * math.pi)
    return (pre_float * cumulative, cumulative + pre_float * density)


def shards(grad_out, pre_act, down_weight):
    shard_rows = grad_out[0]
    token_block = lax.all_gather(shard_rows, "row", axis=0, tiled=True)
    column_block = lax.all_to_all(token_block, "col", split_axis=1, concat_axis=0, tiled=True)
    activated, slope = gelu_parts(pre_act.astype(jnp.float32))
    hidden = activated.astype(jnp.bfloat16)
    row_slice = column_block
    grad_hidden = lax.psum_scatter(
        jnp.dot(row_slice, down_weight, preferred_element_type=jnp.float32),
        "col",
        scatter_dimension=0,
        tiled=True,
    )
    grad_pre = (grad_hidden * slope).astype(jnp.bfloat16)
    row_slice = column_block
    grad_weight = lax.dot_general(
        row_slice,
        lax.all_gather(hidden, "col", axis=0, tiled=True),
        (((0,), (0,)), ((), ())),
        preferred_element_type=jnp.float32,
    )
    return (grad_pre, grad_weight.astype(jnp.bfloat16))


def solution(mesh):
    in_specs = (P("col", "row", None), P("col", "row"), P("col", "row"))
    out_specs = (P("col", "row"), P("col", "row"))
    return jax.shard_map(shards, mesh=mesh, in_specs=in_specs, out_specs=out_specs, check_vma=False)
```

profile of v0, /device:TPU:1, one launch (start us, length us, event | category | flops | bytes accessed | tf_op | source)
XLA Modules:
  0.0 583.2 jit_solution(2370361156632593929)
XLA Ops:
  7.2 0.0 copy-start
  7.2 0.0 all-gather.6.cloned.1.call-start
  7.2 0.7 all-gather.6.cloned.1.call-update
  7.9 0.0 reduce-scatter.2.cloned.1.call-start
  8.0 76.8 %all-gather.6.cloned.1.call-done = bf16[1,256,8192]{2,1,0:T(8,128)(2,1)} async-done(((bf16[1,32,8192]{2,1,0:T(8,128)(2,1)}), bf16[1,256,8192]{2,1,0:T(8,128)(2,1)}) %all-gather.6.cloned.1.call-update) | async-done | bytes 4194320 | tf_op jit(solution)/shard_map/all_gather | solution.py:16
  84.8 6.4 %copy.10 = bf16[1,256,8192]{1,2,0:T(8,128)(2,1)} copy(bf16[1,256,8192]{2,1,0:T(8,128)(2,1)} %all-gather.6.cloned.1.call-done) | data formatting | bytes 8388608 | tf_op jit(solution)/shard_map/all_gather | solution.py:16
  91.1 54.5 %all_to_all.19 = bf16[256,16,512]{0,2,1:T(8,128)(2,1)} all-to-all(bf16[256,16,512]{0,2,1:T(8,128)(2,1)} %bitcast.9), channel_id=1, replica_groups=mesh['row'=8,'col'=16] {'col'}, dimensions={1} | all-to-all | bytes 8388608 | tf_op jit(solution)/shard_map/all_to_all | solution.py:17
  145.7 6.4 %copy.11 = bf16[16,256,512]{2,1,0:T(8,128)(2,1)} copy(bf16[16,256,512]{1,2,0:T(8,128)(2,1)} %bitcast.10) | data formatting | bytes 8388608 | tf_op jit(solution)/shard_map/all_to_all | solution.py:17
  152.0 0.0 copy-done
  152.0 16.4 %fusion.10 = f32[4096,1792]{1,0:T(8,128)} fusion(bf16[4096,512]{1,0:T(8,128)(2,1)} %bitcast.11, bf16[512,1792]{1,0:T(8,128)(2,1)S(1)} %copy-done), kind=kOutput, calls=%fused_computation.16 | convolution fusion | flops 7516192768 | bytes 35389440 | tf_op jit(solution)/shard_map/dot_general | solution.py:22
  168.4 0.0 copy-start.2
  168.4 0.0 reduce-scatter.2.cloned.1.call-update
  168.5 0.0 all-gather.4.cloned.1.call-start
  168.5 305.0 %reduce-scatter.2.cloned.1.call-done = f32[256,1792]{1,0:T(8,128)} async-done(((f32[4096,1792]{1,0:T(8,128)}), f32[256,1792]{1,0:T(8,128)}) %reduce-scatter.2.cloned.1.call-update) | async-done | bytes 1835024 | tf_op jit(solution)/shard_map/reduce_scatter | solution.py:21
  473.5 0.0 copy-done.2
  473.5 3.6 fusion.9
  477.1 0.0 all-gather.4.cloned.1.call-update
  477.1 82.4 %all-gather.4.cloned.1.call-done = bf16[4096,1792]{1,0:T(8,128)(2,1)} async-done(((bf16[256,1792]{1,0:T(8,128)(2,1)}), bf16[4096,1792]{1,0:T(8,128)(2,1)}) %all-gather.4.cloned.1.call-update) | async-done | bytes 14680080 | tf_op jit(solution)/shard_map/all_gather | solution.py:31
  559.5 0.0 copy-start.1
  559.5 13.3 %fusion = bf16[512,1792]{0,1:T(8,128)(2,1)} fusion(bf16[4096,1792]{1,0:T(8,128)(2,1)} %all-gather.4.cloned.1.call-done, bf16[4096,512]{1,0:T(8,128)(2,1)} %bitcast.12), kind=kOutput, calls=%fused_computation.6 | convolution fusion | flops 7517110272 | bytes 20709376 | tf_op jit(solution)/shard_map/dot_general | solution.py:29
  572.9 3.8 copy.12
  576.7 0.0 copy-done.1
Async XLA Ops:
  7.2 144.9 %copy-start = (bf16[512,1792]{1,0:T(8,128)(2,1)S(1)}, bf16[512,1792]{1,0:T(8,128)(2,1)}, u32[]{:S(2)}) copy-start(bf16[512,1792]{1,0:T(8,128)(2,1)} %param.5) | copy-start | bytes 5505028
  7.2 77.6 %all-gather.6.cloned.1.call-start = ((), (), s32[]{:S(2)}) async-start(), calls=%async_computation.4 | async-start | bytes 4718592 | tf_op jit(solution)/shard_map/all_gather | solution.py:16
  7.9 465.6 %reduce-scatter.2.cloned.1.call-start = ((), (), s32[]{:S(2)}) async-start(), calls=%async_computation.2 | async-start | bytes 31195136 | tf_op jit(solution)/shard_map/reduce_scatter | solution.py:21
  168.4 305.0 %copy-start.2 = (bf16[256,1792]{1,0:T(8,128)(2,1)S(1)}, bf16[256,1792]{1,0:T(8,128)(2,1)}, u32[]{:S(2)}) copy-start(bf16[256,1792]{1,0:T(8,128)(2,1)} %param.4) | copy-start | bytes 2752516
  168.5 391.1 %all-gather.4.cloned.1.call-start = ((), (), s32[]{:S(2)}) async-start(), calls=%async_computation.3 | async-start | bytes 15597568 | tf_op jit(solution)/shard_map/all_gather | solution.py:31
  559.5 17.1 %copy-start.1 = (bf16[512,1792]{1,0:T(8,128)(2,1)S(1)}, bf16[512,1792]{1,0:T(8,128)(2,1)}, u32[]{:S(2)}) copy-start(bf16[512,1792]{1,0:T(8,128)(2,1)} %param.5) | copy-start | bytes 5505028
Sparse Core Ops, SparseCore 0:
  10.4 74.3 all-gather.5
  168.6 304.8 reduce-scatter.1
  477.2 82.2 all-gather.3
where the time goes:
time: 584 us; the launch traced here: 583 us
  waiting for transfers between devices  465 us (80%)
  blocking collectives  54.5 us (9%)
  matrix products  29.7 us (5%)
  local copies, waits for them, and re-layouts  16.5 us (3%)
  between operations  13.8 us (2%)
    reduce_scatter x1, waiting for transfers between devices, shards(): lax.psum_scatter(jnp.dot(row_slice, down_weight, preferred_element_type=j...  305 us
    all_gather x1, waiting for transfers between devices, shards(): lax.all_gather(hidden, 'col', axis=0, tiled=True)  82.4 us
    all_gather x1, waiting for transfers between devices, shards(): token_block = lax.all_gather(shard_rows, 'row', axis=0, tiled=True)  76.8 us
    all_to_all x1, blocking collectives, shards(): lax.all_to_all(token_block, 'col', split_axis=1, concat_axis=0, tiled=True)  54.5 us
    dot_general x1, matrix products, shards(): jnp.dot(row_slice, down_weight, preferred_element_type=jnp.float32)  16.4 us
    dot_general x1, matrix products, shards(): lax.dot_general(row_slice, lax.all_gather(hidden, 'col', axis=0, tiled=Tr...  13.3 us
  transfers between devices with their start and end apart: 3, of which 3 were waited for; matrix products, arithmetic and copies ran while one was open for 0% of the time, Pallas kernels for 0%

commit v1 on v0

--- a/solution.py
+++ b/solution.py
@@ -13,7 +13,9 @@
 
 def shards(grad_out, pre_act, down_weight):
     shard_rows = grad_out[0]
-    token_block = lax.all_gather(shard_rows, "row", axis=0, tiled=True)
+    token_block = jnp.concatenate(
+        jax.lax.all_to_all(jnp.stack([shard_rows] * jax.lax.psum(1, "row")), "row", 0, 0), axis=0
+    )
     column_block = lax.all_to_all(token_block, "col", split_axis=1, concat_axis=0, tiled=True)
     activated, slope = gelu_parts(pre_act.astype(jnp.float32))
     hidden = activated.astype(jnp.bfloat16)

time: 584 us -> 557 us (0.954)
  waiting for transfers between devices: 465 us -> 387 us
  blocking collectives: 54.5 us -> 113 us
    all_gather x1 -> x0, waiting for transfers between devices: 76.8 us -> none  [shards(): token_block = lax.all_gather(shard_rows, 'row', axis=0, tiled=True)]
    all_to_all x0 -> x1, blocking collectives: none -> 57.2 us  [shards(): jax.lax.all_to_all(jnp.stack([shard_rows] * jax.lax.psum(1, 'row')), 'row...]
    all_gather x1 -> x0, local copies, waits for them, and re-layouts: 6.36 us -> none  [shards(): token_block = lax.all_gather(shard_rows, 'row', axis=0, tiled=True)]
  transfers between devices with their start and end apart: 3 -> 2, of which waited for: 3 -> 2; matrix products, arithmetic and copies ran while one was open for 0% -> 0% of each run, Pallas kernels for 0% -> 0%
where the time goes in v1:
time: 557 us; the launch traced here: 556 us
  waiting for transfers between devices  387 us (69%)
  blocking collectives  113 us (20%)
  matrix products  26.2 us (5%)
  between operations  14.1 us (3%)
  local copies, waits for them, and re-layouts  11.6 us (2%)
    reduce_scatter x1, waiting for transfers between devices, shards(): lax.psum_scatter(jnp.dot(row_slice, down_weight, preferred_element_type=j...  305 us
    all_gather x1, waiting for transfers between devices, shards(): lax.all_gather(hidden, 'col', axis=0, tiled=True)  82.4 us
    all_to_all x1, blocking collectives, shards(): jax.lax.all_to_all(jnp.stack([shard_rows] * jax.lax.psum(1, 'row')), 'row...  57.2 us
    all_to_all x1, blocking collectives, shards(): lax.all_to_all(token_block, 'col', split_axis=1, concat_axis=0, tiled=True)  56.2 us
    dot_general x1, matrix products, shards(): lax.dot_general(row_slice, lax.all_gather(hidden, 'col', axis=0, tiled=Tr...  13.3 us
    dot_general x1, matrix products, shards(): jnp.dot(row_slice, down_weight, preferred_element_type=jnp.float32)  12.9 us
  transfers between devices with their start and end apart: 2, of which 2 were waited for; matrix products, arithmetic and copies ran while one was open for 0% of the time, Pallas kernels for 0%

profile of v1, /device:TPU:1, one launch (start us, length us, event | category | flops | bytes accessed | tf_op | source)
XLA Modules:
  0.0 556.3 jit_solution(7176272466250472927)
XLA Ops:
  7.2 0.0 copy-start
  7.2 0.0 reduce-scatter.2.cloned.1.call-start
  7.2 1.6 stack.3
  8.9 57.2 %all_to_all.24 = bf16[8,32,8192]{2,1,0:T(8,128)(2,1)S(1)} all-to-all(bf16[8,32,8192]{2,1,0:T(8,128)(2,1)S(1)} %stack.3), channel_id=1, replica_groups=mesh['row'=8,'col'=16] {'row'}, dimensions={0} | all-to-all | bytes 8388608 | tf_op jit(solution)/shard_map/all_to_all | solution.py:17
  66.1 1.9 copy.11
  67.9 2.4 copy.9
  70.3 56.2 %all_to_all.25 = bf16[256,16,512]{2,0,1:T(8,128)(2,1)S(1)} all-to-all(bf16[256,16,512]{2,0,1:T(8,128)(2,1)S(1)} %copy.9), channel_id=1, replica_groups=mesh['row'=8,'col'=16] {'col'}, dimensions={1} | all-to-all | bytes 8388608 | tf_op jit(solution)/shard_map/all_to_all | solution.py:19
  126.5 0.0 copy-start.2
  126.5 1.9 copy-done.2
  128.4 0.0 copy-done
  128.4 12.9 %fusion.10 = f32[4096,1792]{1,0:T(8,128)} fusion(bf16[4096,512]{1,0:T(8,128)(2,1)S(1)} %bitcast.15, bf16[512,1792]{1,0:T(8,128)(2,1)S(1)} %copy-done), kind=kOutput, calls=%fused_computation.16 | convolution fusion | flops 7516192768 | bytes 35389440 | tf_op jit(solution)/shard_map/dot_general | solution.py:24
  141.3 0.0 copy-start.3
  141.3 0.0 reduce-scatter.2.cloned.1.call-update
  141.3 0.0 all-gather.2.cloned.1.call-start
  141.4 305.0 %reduce-scatter.2.cloned.1.call-done = f32[256,1792]{1,0:T(8,128)} async-done(((f32[4096,1792]{1,0:T(8,128)}), f32[256,1792]{1,0:T(8,128)}) %reduce-scatter.2.cloned.1.call-update) | async-done | bytes 1835024 | tf_op jit(solution)/shard_map/reduce_scatter | solution.py:23
  446.3 0.0 copy-done.3
  446.3 3.6 fusion.9
  449.9 0.0 all-gather.2.cloned.1.call-update
  450.0 82.4 %all-gather.2.cloned.1.call-done = bf16[4096,1792]{1,0:T(8,128)(2,1)} async-done(((bf16[256,1792]{1,0:T(8,128)(2,1)}), bf16[4096,1792]{1,0:T(8,128)(2,1)}) %all-gather.2.cloned.1.call-update) | async-done | bytes 14680080 | tf_op jit(solution)/shard_map/all_gather | solution.py:33
  532.4 0.0 copy-start.1
  532.4 13.3 %fusion = bf16[512,1792]{0,1:T(8,128)(2,1)} fusion(bf16[4096,1792]{1,0:T(8,128)(2,1)} %all-gather.2.cloned.1.call-done, bf16[4096,512]{1,0:T(8,128)(2,1)} %bitcast.16), kind=kOutput, calls=%fused_computation.6 | convolution fusion | flops 7517110272 | bytes 20709376 | tf_op jit(solution)/shard_map/dot_general | solution.py:31
  545.7 3.8 copy.10
  549.5 0.0 copy-done.1
Async XLA Ops:
  7.2 121.3 %copy-start = (bf16[512,1792]{1,0:T(8,128)(2,1)S(1)}, bf16[512,1792]{1,0:T(8,128)(2,1)}, u32[]{:S(2)}) copy-start(bf16[512,1792]{1,0:T(8,128)(2,1)} %param.5) | copy-start | bytes 5505028
  7.2 439.1 %reduce-scatter.2.cloned.1.call-start = ((), (), s32[]{:S(2)}) async-start(), calls=%async_computation.3 | async-start | bytes 31195136 | tf_op jit(solution)/shard_map/reduce_scatter | solution.py:23
  126.5 1.9 copy-start.2
  141.3 305.0 %copy-start.3 = (bf16[256,1792]{1,0:T(8,128)(2,1)S(1)}, bf16[256,1792]{1,0:T(8,128)(2,1)}, u32[]{:S(2)}) copy-start(bf16[256,1792]{1,0:T(8,128)(2,1)} %param.4) | copy-start | bytes 2752516
  141.3 391.1 %all-gather.2.cloned.1.call-start = ((), (), s32[]{:S(2)}) async-start(), calls=%async_computation.4 | async-start | bytes 15597568 | tf_op jit(solution)/shard_map/all_gather | solution.py:33
  532.4 17.1 %copy-start.1 = (bf16[512,1792]{1,0:T(8,128)(2,1)S(1)}, bf16[512,1792]{1,0:T(8,128)(2,1)}, u32[]{:S(2)}) copy-start(bf16[512,1792]{1,0:T(8,128)(2,1)} %param.5) | copy-start | bytes 5505028
Sparse Core Ops, SparseCore 0:
  141.4 304.8 reduce-scatter.1
  450.1 82.2 all-gather.1
